TPU v7x, 32 devices: a whole 2x2x4 slice. The times are simulated.
32 devices in a mesh: groups: 2 (over x), col: 16 (over z, y, core).
Axes of the slice: x: 2, y: 2, z: 4, core: 2. Of those that a mesh axis runs over, the one named last changes fastest.
Arguments:
- slab: float32 [2, 2048, 4096], P(None, 'groups', 'col'), parts along dimension 1, may hold values from -6 to 6
- block_on: int32 [16, 32], P('groups', 'col'), parts along dimension 0, may hold values 0 or 1
- block_band: int32 [16, 32], P('groups', 'col'), parts along dimension 0, may hold values from 0 to 3
- band_gain: float32 [4], replicated, may hold values from 0.25 to 2
Outputs:
- spectra: float32 [2, 2048, 4096], P(None, 'groups', 'col'), parts along dimension 1
There are 2 independent parts, one for each index of `groups`. A program takes and returns all parts, laid end to end along the dimension named above; an argument that names none is the same for every part. Nothing has to cross between parts.
All inputs are finite; a program needn't handle non-finite values. No bound on the sum of `block_on` on one device may be relied on, other than what follows from the above.
Results may differ from a plain program's by a relative error of at most 0.00007.
Values sent between devices are 32-bit elements; how exact they have to be, the bound alone decides.
No kernel may reach another device: no remote copies, remote signals or barrier semaphores. Data moves between devices by JAX's collectives and lax.ppermute only.
A program may use at most 64 MiB of HBM per device.

v0:
```python
import math
import jax
import jax.numpy as jnp
from jax import lax
from jax.sharding import PartitionSpec as P

BLOCK = 128


def phase_table(first_index, second_index, length):
    product = first_index[:, None] * second_index[None, :] % length
    angles = product.astype(jnp.float32) * (2.0 * math.pi / length)
    return (jnp.cos(angles), -jnp.sin(angles))


def contract(stacked, table, formula):
    cosine_table, sine_table = table
    real_part = jnp.einsum(
        formula, stacked[0], cosine_table, precision=lax.Precision.HIGHEST
    ) - jnp.einsum(formula, stacked[1], sine_table, precision=lax.Precision.HIGHEST)
    imag_part = jnp.einsum(
        formula, stacked[0], sine_table, precision=lax.Precision.HIGHEST
    ) + jnp.einsum(formula, stacked[1], cosine_table, precision=lax.Precision.HIGHEST)
    return jnp.stack([real_part, imag_part])


def rotate(stacked, table):
    cosine_table, sine_table = table
    real_part = stacked[0] * cosine_table - stacked[1] * sine_table
    imag_part = stacked[0] * sine_table + stacked[1] * cosine_table
    return jnp.stack([real_part, imag_part])


def shards(slab, block_on, block_band, band_gain):
    devices = lax.axis_size("col")
    rows_total = slab.shape[1]
    shard_cols = slab.shape[2]
    length = shard_cols * devices
    rows_here = rows_total // devices
    factor = 1.0 / math.sqrt(length)
    first_len = BLOCK
    second_len = length // first_len
    first_iota = jnp.arange(first_len, dtype=jnp.int32)
    second_iota = jnp.arange(second_len, dtype=jnp.int32)
    table_one = phase_table(first_iota, first_iota, first_len)
    table_middle = phase_table(first_iota, second_iota, length)
    table_two = phase_table(second_iota, second_iota, second_len)
    received = lax.all_to_all(
        slab.reshape(2, devices, rows_here, shard_cols),
        "col",
        split_axis=1,
        concat_axis=3,
        tiled=True,
    )
    row_count = received.shape[2]
    square = received[:, 0].reshape(2, row_count, first_len, second_len)
    mixture = contract(square, table_one, "rab,ak->rkb")
    mixture = rotate(mixture, table_middle)
    result = contract(mixture, table_two, "rkb,bm->rmk")
    whole = result.reshape(2, 1, row_count, length)
    whole = whole.reshape(2, rows_here, devices, shard_cols)
    spectrum = lax.all_to_all(whole, "col", split_axis=2, concat_axis=1, tiled=True).reshape(
        2, rows_total, shard_cols
    )
    choose = (block_band[..., None] == jnp.arange(band_gain.shape[0], dtype=jnp.int32)).astype(
        jnp.float32
    )
    weight = block_on.astype(jnp.float32) * jnp.sum(choose * band_gain, axis=-1) * factor
    row_blocks = rows_total // BLOCK
    col_blocks = shard_cols // BLOCK
    masked = (
        spectrum.reshape(2, row_blocks, BLOCK, col_blocks, BLOCK) * weight[None, :, None, :, None]
    )
    return masked.reshape(2, rows_total, shard_cols)


def solution(mesh):
    placed = (P(None, "groups", "col"), P("groups", "col"), P("groups", "col"), P())
    return jax.shard_map(
        shards, mesh=mesh, in_specs=placed, out_specs=P(None, "groups", "col"), check_vma=False
    )
```

profile of v0, /device:TPU:13, one launch (start us, length us, event | category | flops | bytes accessed | tf_op | source)
XLA Modules:
  0.0 138.4 jit_solution(2403043482625478237)
XLA Ops:
  0.0 3.1 %copy.54 = f32[2,16,64,256]{3,2,0,1:T(8,128)} copy(f32[2,16,64,256]{3,2,1,0:T(8,128)} %bitcast.56) | data formatting | bytes 4194304 | tf_op jit(solution)/shard_map/reshape | solution.py:49
  3.1 6.5 %all-to-all-start = ((f32[2,16,64,256]{3,2,0,1:T(8,128)}), f32[2,16,64,256]{3,2,0,1:T(8,128)S(1)}, u32[]{:S(2)}, u32[]{:S(2)}) async-start(f32[2,16,64,256]{3,2,0,1:T(8,128)} %copy.54), calls=%async_computation | async-start | bytes 4194304 | tf_op jit(solution)/shard_map/all_to_all | solution.py:48
  9.7 0.1 sine_negate_fusion.4
  9.7 47.3 %all-to-all-done = f32[2,16,64,256]{3,2,0,1:T(8,128)S(1)} async-done(((f32[2,16,64,256]{3,2,0,1:T(8,128)}), f32[2,16,64,256]{3,2,0,1:T(8,128)S(1)}, u32[]{:S(2)}, u32[]{:S(2)}) %all-to-all-start) | async-done | bytes 2097184 | tf_op jit(solution)/shard_map/all_to_all | solution.py:48
  57.1 1.2 fusion.79
  58.2 0.6 copy.55
  58.8 1.3 copy.56
  60.1 1.2 fusion.11
  61.4 2.2 %fusion.15 = f32[128,64,32]{0,1,2:T(8,128)} fusion(f32[64,128,32]{1,0,2:T(8,128)S(1)} %copy.56), kind=kOutput, calls=%fused_computation.27 | convolution fusion | flops 402882560 | bytes 2097152 | tf_op jit(solution)/shard_map/rab,ak->rkb/dot_general | solution.py:18
  63.6 1.9 %copy.57 = f32[1,1,64,16,256]{2,4,3,1,0:T(8,128)} copy(f32[1,1,64,16,256]{4,2,0,3,1:T(8,128)S(1)} %copy-done.1) | data formatting | bytes 2097152 | tf_op jit(solution)/shard_map/slice | solution.py:20
  65.5 2.7 %copy.58 = f32[64,128,32]{1,0,2:T(8,128)S(1)} copy(f32[64,128,32]{0,2,1:T(8,128)} %bitcast.52) | data formatting | bytes 2097152 | tf_op jit(solution)/shard_map/squeeze | solution.py:20
  68.2 0.0 copy-start
  68.2 1.3 convolution_add_fusion.1
  69.5 1.4 %add_bitcast_fusion = (f32[64,128,32]{1,0,2:T(8,128)S(1)}, f32[64,128,32]{1,0,2:T(8,128)S(1)}) fusion(f32[128,64,32]{0,1,2:T(8,128)S(1)} %convolution_add_fusion.1, f32[128,32]{0,1:T(8,128)S(1)} %get-tuple-element.9, f32[128,32]{0,1:T(8,128)S(1)} %get-tuple-element.10, f32[128,64,32]{0,1,2:T(8,128)S(1)} %copy-done, f32[64,128,32]{1,0,2:T(8,128)S(1)} %copy.58), kind=kOutput, calls=%fused_computation.9 | convolution fusion | flops 404733952 | bytes 5275648 | tf_op jit(solution)/shard_map/rab,ak->rkb/dot_general | solution.py:20
  70.9 1.6 %fusion.6 = f32[32,64,128]{2,0,1:T(8,128)S(1)} fusion(f32[64,128,32]{1,0,2:T(8,128)S(1)} %get-tuple-element.6), kind=kOutput, calls=%fused_computation.15 | convolution fusion | flops 100677632 | bytes 2097152 | tf_op jit(solution)/shard_map/rkb,bm->rmk/dot_general | solution.py:18
  72.5 1.6 %fusion.4 = f32[32,64,128]{2,0,1:T(8,128)S(1)} fusion(f32[64,128,32]{1,0,2:T(8,128)S(1)} %get-tuple-element.6), kind=kOutput, calls=%fused_computation.13 | convolution fusion | flops 100678656 | bytes 2097152 | tf_op jit(solution)/shard_map/rkb,bm->rmk/dot_general | solution.py:21
  74.1 1.8 %fusion.1 = f32[64,32,128]{2,1,0:T(8,128)S(1)} fusion(f32[32,64,128]{2,0,1:T(8,128)S(1)} %fusion.6, f32[64,128,32]{1,0,2:T(8,128)S(1)} %get-tuple-element.5), kind=kOutput, calls=%fused_computation.5 | convolution fusion | flops 100940800 | bytes 3145728 | tf_op jit(solution)/shard_map/rkb,bm->rmk/dot_general | solution.py:20
  75.9 1.3 stack.9
  77.1 2.8 %copy.65 = f32[1,64,16,256]{3,1,0,2:T(8,128)} copy(f32[1,64,16,256]{3,2,1,0:T(8,128)} %stack.9) | data formatting | bytes 2097152 | tf_op jit(solution)/shard_map/stack | solution.py:24
  79.9 1.6 %fusion = f32[64,32,128]{2,1,0:T(8,128)S(1)} fusion(f32[32,64,128]{2,0,1:T(8,128)S(1)} %fusion.4, f32[64,128,32]{1,0,2:T(8,128)S(1)} %get-tuple-element.5), kind=kOutput, calls=%fused_computation.3 | convolution fusion | flops 100939776 | bytes 3145728 | tf_op jit(solution)/shard_map/rkb,bm->rmk/dot_general | solution.py:23
  81.6 0.3 stack.10
  81.9 0.6 copy.66
  82.5 0.3 copy-done.2
  82.8 1.5 %pad_maximum_fusion = f32[2,64,16,256]{3,1,0,2:T(8,128)} fusion(f32[1,64,16,256]{3,1,0,2:T(8,128)S(1)} %copy.66, f32[1,64,16,256]{3,1,0,2:T(8,128)S(1)} %copy-done.2), kind=kLoop, calls=%fused_computation | loop fusion | flops 524288 | bytes 4194304 | tf_op jit(solution)/shard_map/stack | solution.py:24
  84.2 4.9 %all-to-all-start.1 = ((f32[2,64,16,256]{3,1,0,2:T(8,128)}), f32[2,64,16,256]{3,1,0,2:T(8,128)S(1)}, u32[]{:S(2)}, u32[]{:S(2)}) async-start(f32[2,64,16,256]{3,1,0,2:T(8,128)} %pad_maximum_fusion), calls=%async_computation.1 | async-start | bytes 4194304 | tf_op jit(solution)/shard_map/all_to_all | solution.py:62
  89.2 0.1 select_reduce_fusion
  89.3 0.1 copy.68
  89.4 0.3 mul.231
  89.7 0.1 copy.79
  89.8 46.8 %all-to-all-done.1 = f32[2,64,16,256]{3,1,0,2:T(8,128)S(1)} async-done(((f32[2,64,16,256]{3,1,0,2:T(8,128)}), f32[2,64,16,256]{3,1,0,2:T(8,128)S(1)}, u32[]{:S(2)}, u32[]{:S(2)}) %all-to-all-start.1) | async-done | bytes 2097184 | tf_op jit(solution)/shard_map/all_to_all | solution.py:62
  136.6 0.2 copy.67
  136.8 1.5 %bitcast_multiply_fusion = f32[2,1024,256]{2,1,0:T(8,128)} fusion(f32[2,64,16,256]{3,1,2,0:T(8,128)S(1)} %copy.67, f32[1024,256]{1,0:T(8,128)S(1)} %bitcast.54), kind=kLoop, calls=%fused_computation.1 | loop fusion | flops 524288 | bytes 5242880 | tf_op jit(solution)/shard_map/mul | solution.py:72
  (11 shorter events, 0.0 us)
Async XLA Ops:
  3.1 53.9 %all-to-all-start = ((f32[2,16,64,256]{3,2,0,1:T(8,128)}), f32[2,16,64,256]{3,2,0,1:T(8,128)S(1)}, u32[]{:S(2)}, u32[]{:S(2)}) async-start(f32[2,16,64,256]{3,2,0,1:T(8,128)} %copy.54), calls=%async_computation | async-start | bytes 4194304 | tf_op jit(solution)/shard_map/all_to_all | solution.py:48
  60.1 3.5 %copy-start.1 = (f32[1,1,64,16,256]{4,2,0,3,1:T(8,128)S(1)}, f32[1,1,64,16,256]{4,2,0,3,1:T(8,128)}, u32[]{:S(2)}) copy-start(f32[1,1,64,16,256]{4,2,0,3,1:T(8,128)} %get-tuple-element.7) | copy-start | bytes 3145732
  68.2 1.3 copy-start
  81.5 1.2 copy-start.2
  84.2 5.0 %copy-start.4 = (s32[8,2]{0,1:T(2,128)S(1)}, s32[8,2]{0,1:T(2,128)}, u32[]{:S(2)}) copy-start(s32[8,2]{0,1:T(2,128)} %param.6) | copy-start | bytes 196
  84.2 5.0 %copy-start.5 = (f32[4]{0:T(128)S(1)}, f32[4]{0:T(128)}, u32[]{:S(2)}) copy-start(f32[4]{0:T(128)} %param.7) | copy-start | bytes 52
  84.2 5.0 %copy-start.3 = (s32[8,2]{0,1:T(2,128)S(1)}, s32[8,2]{0,1:T(2,128)}, u32[]{:S(2)}) copy-start(s32[8,2]{0,1:T(2,128)} %param.5) | copy-start | bytes 196
  84.2 52.4 %all-to-all-start.1 = ((f32[2,64,16,256]{3,1,0,2:T(8,128)}), f32[2,64,16,256]{3,1,0,2:T(8,128)S(1)}, u32[]{:S(2)}, u32[]{:S(2)}) async-start(f32[2,64,16,256]{3,1,0,2:T(8,128)} %pad_maximum_fusion), calls=%async_computation.1 | async-start | bytes 4194304 | tf_op jit(solution)/shard_map/all_to_all | solution.py:62
where the time goes:
time: 139 us; the launch traced here: 138 us
  waiting for transfers between devices  94.1 us (68%)
  local copies, waits for them, and re-layouts  16.8 us (12%)
  matrix products  12.7 us (9%)
  starting transfers between devices  11.5 us (8%)
  other arithmetic  3.18 us (2%)
    all_to_all x1, waiting for transfers between devices, shards(): lax.all_to_all(slab.reshape(2, devices, rows_here, shard_cols), 'col', sp...  47.3 us
    all_to_all x1, waiting for transfers between devices, shards(): lax.all_to_all(whole, 'col', split_axis=2, concat_axis=1, tiled=True)  46.8 us
    all_to_all x1, starting transfers between devices, shards(): lax.all_to_all(slab.reshape(2, devices, rows_here, shard_cols), 'col', sp...  6.52 us
    another operation x4, local copies, waits for them, and re-layouts, contract(): return jnp.stack([real_part, imag_part])  4.98 us
    all_to_all x1, starting transfers between devices, shards(): lax.all_to_all(whole, 'col', split_axis=2, concat_axis=1, tiled=True)  4.94 us
    dot_general x2, matrix products, contract(): jnp.einsum(formula, stacked[0], cosine_table, precision=lax.Precision.HIG...  3.8 us
    dot_general x2, matrix products, contract(): jnp.einsum(formula, stacked[1], sine_table, precision=lax.Precision.HIGHEST)  3.18 us
    reshape x1, local copies, waits for them, and re-layouts, shards(): slab.reshape(2, devices, rows_here, shard_cols)  3.13 us
  transfers between devices with their start and end apart: 2, of which 2 were waited for; matrix products, arithmetic and copies ran while one was open for 0% of the time, Pallas kernels for 0%

commit v1 on v0

--- a/solution.py
+++ b/solution.py
@@ -45,13 +45,10 @@
     table_one = phase_table(first_iota, first_iota, first_len)
     table_middle = phase_table(first_iota, second_iota, length)
     table_two = phase_table(second_iota, second_iota, second_len)
-    received = lax.all_to_all(
-        slab.reshape(2, devices, rows_here, shard_cols),
-        "col",
-        split_axis=1,
-        concat_axis=3,
-        tiled=True,
-    )
+    block = slab.reshape(2, devices, rows_here, shard_cols)
+    pieces = jnp.split(block, lax.axis_size("col"), axis=1)
+    incoming = lax.all_to_all(jnp.stack(pieces), "col", 0, 0)
+    received = jnp.concatenate(incoming, axis=3)
     row_count = received.shape[2]
     square = received[:, 0].reshape(2, row_count, first_len, second_len)
     mixture = contract(square, table_one, "rab,ak->rkb")

time: 139 us -> 145 us (1.043)
  local copies, waits for them, and re-layouts: 16.8 us -> 22.6 us
    unnamed x13 -> x32, local copies, waits for them, and re-layouts: 0.39 us -> 9.3 us
    reshape x1 -> x0, local copies, waits for them, and re-layouts: 3.13 us -> none  [shards(): slab.reshape(2, devices, rows_here, shard_cols)]
where the time goes in v1:
time: 145 us; the launch traced here: 144 us
  waiting for transfers between devices  94.1 us (65%)
  local copies, waits for them, and re-layouts  22.6 us (16%)
  matrix products  12.7 us (9%)
  starting transfers between devices  11.4 us (8%)
  other arithmetic  3.18 us (2%)
    all_to_all x1, waiting for transfers between devices, shards(): incoming = lax.all_to_all(jnp.stack(pieces), 'col', 0, 0)  47.3 us
    all_to_all x1, waiting for transfers between devices, shards(): lax.all_to_all(whole, 'col', split_axis=2, concat_axis=1, tiled=True)  46.8 us
    unnamed x32, local copies, waits for them, and re-layouts  9.3 us
    all_to_all x1, starting transfers between devices, shards(): incoming = lax.all_to_all(jnp.stack(pieces), 'col', 0, 0)  6.52 us
    another operation x4, local copies, waits for them, and re-layouts, contract(): return jnp.stack([real_part, imag_part])  4.98 us
    all_to_all x1, starting transfers between devices, shards(): lax.all_to_all(whole, 'col', split_axis=2, concat_axis=1, tiled=True)  4.91 us
    dot_general x2, matrix products, contract(): jnp.einsum(formula, stacked[0], cosine_table, precision=lax.Precision.HIG...  3.8 us
    dot_general x2, matrix products, contract(): jnp.einsum(formula, stacked[1], sine_table, precision=lax.Precision.HIGHEST)  3.18 us
  transfers between devices with their start and end apart: 2, of which 2 were waited for; matrix products, arithmetic and copies ran while one was open for 0% of the time, Pallas kernels for 0%

profile of v1, /device:TPU:13, one launch (start us, length us, event | category | flops | bytes accessed | tf_op | source)
XLA Modules:
  0.0 144.2 jit_solution(10742335879080661850)
XLA Ops:
  0.0 1.1 fusion.23
  1.1 0.9 fusion.22
  2.0 0.9 fusion.21
  2.9 0.9 fusion.20
  3.8 0.9 fusion.19
  4.8 0.9 fusion.18
  5.7 0.9 fusion.17
  6.6 0.9 fusion.16
  7.7 1.3 copy-done.3
  9.0 6.5 %all-to-all-start = ((f32[16,2,1,64,256]{4,3,2,1,0:T(8,128)}), f32[16,2,1,64,256]{4,3,2,1,0:T(8,128)S(1)}, u32[]{:S(2)}, u32[]{:S(2)}) async-start(f32[16,2,1,64,256]{4,3,2,1,0:T(8,128)} %bitcast.149), calls=%async_computation | async-start | bytes 4194304 | tf_op jit(solution)/shard_map/all_to_all | solution.py:50
  15.6 47.3 %all-to-all-done = f32[16,2,1,64,256]{4,3,2,1,0:T(8,128)S(1)} async-done(((f32[16,2,1,64,256]{4,3,2,1,0:T(8,128)}), f32[16,2,1,64,256]{4,3,2,1,0:T(8,128)S(1)}, u32[]{:S(2)}, u32[]{:S(2)}) %all-to-all-start) | async-done | bytes 2097184 | tf_op jit(solution)/shard_map/all_to_all | solution.py:50
  63.0 1.2 fusion.95
  64.1 0.6 copy.130
  64.7 1.3 copy.131
  66.0 1.2 fusion.27
  67.3 2.2 %fusion.31 = f32[128,64,32]{0,1,2:T(8,128)} fusion(f32[64,128,32]{1,0,2:T(8,128)S(1)} %copy.131), kind=kOutput, calls=%fused_computation.59 | convolution fusion | flops 402882560 | bytes 2097152 | tf_op jit(solution)/shard_map/rab,ak->rkb/dot_general | solution.py:18
  69.5 1.9 %copy.132 = f32[1,1,64,16,256]{2,4,3,1,0:T(8,128)} copy(f32[1,1,64,16,256]{4,2,1,0,3:T(8,128)S(1)} %copy-done.1) | data formatting | bytes 2097152 | tf_op jit(solution)/shard_map/slice | solution.py:20
  71.4 2.7 %copy.133 = f32[64,128,32]{1,0,2:T(8,128)S(1)} copy(f32[64,128,32]{0,2,1:T(8,128)} %bitcast.145) | data formatting | bytes 2097152 | tf_op jit(solution)/shard_map/squeeze | solution.py:20
  74.1 1.3 convolution_add_fusion.1
  75.4 1.4 add_bitcast_fusion
  76.8 1.6 %fusion.6 = f32[32,64,128]{2,0,1:T(8,128)S(1)} fusion(f32[64,128,32]{1,0,2:T(8,128)S(1)} %get-tuple-element.6), kind=kOutput, calls=%fused_computation.15 | convolution fusion | flops 100677632 | bytes 2097152 | tf_op jit(solution)/shard_map/rkb,bm->rmk/dot_general | solution.py:18
  78.4 1.6 %fusion.4 = f32[32,64,128]{2,0,1:T(8,128)S(1)} fusion(f32[64,128,32]{1,0,2:T(8,128)S(1)} %get-tuple-element.6), kind=kOutput, calls=%fused_computation.13 | convolution fusion | flops 100678656 | bytes 2097152 | tf_op jit(solution)/shard_map/rkb,bm->rmk/dot_general | solution.py:21
  80.0 1.8 %fusion.1 = f32[64,32,128]{2,1,0:T(8,128)S(1)} fusion(f32[32,64,128]{2,0,1:T(8,128)S(1)} %fusion.6, f32[64,128,32]{1,0,2:T(8,128)S(1)} %get-tuple-element.5), kind=kOutput, calls=%fused_computation.5 | convolution fusion | flops 100940800 | bytes 3145728 | tf_op jit(solution)/shard_map/rkb,bm->rmk/dot_general | solution.py:20
  81.8 1.3 stack.77
  83.0 2.8 %copy.140 = f32[1,64,16,256]{3,1,0,2:T(8,128)} copy(f32[1,64,16,256]{3,2,1,0:T(8,128)} %stack.77) | data formatting | bytes 2097152 | tf_op jit(solution)/shard_map/stack | solution.py:24
  85.8 1.6 %fusion = f32[64,32,128]{2,1,0:T(8,128)S(1)} fusion(f32[32,64,128]{2,0,1:T(8,128)S(1)} %fusion.4, f32[64,128,32]{1,0,2:T(8,128)S(1)} %get-tuple-element.5), kind=kOutput, calls=%fused_computation.3 | convolution fusion | flops 100939776 | bytes 3145728 | tf_op jit(solution)/shard_map/rkb,bm->rmk/dot_general | solution.py:23
  87.8 0.6 copy.141
  88.7 1.5 %pad_maximum_fusion = f32[2,64,16,256]{3,1,0,2:T(8,128)} fusion(f32[1,64,16,256]{3,1,0,2:T(8,128)S(1)} %copy.141, f32[1,64,16,256]{3,1,0,2:T(8,128)S(1)} %copy-done.2), kind=kLoop, calls=%fused_computation | loop fusion | flops 524288 | bytes 4194304 | tf_op jit(solution)/shard_map/stack | solution.py:24
  90.2 4.9 %all-to-all-start.1 = ((f32[2,64,16,256]{3,1,0,2:T(8,128)}), f32[2,64,16,256]{3,1,0,2:T(8,128)S(1)}, u32[]{:S(2)}, u32[]{:S(2)}) async-start(f32[2,64,16,256]{3,1,0,2:T(8,128)} %pad_maximum_fusion), calls=%async_computation.1 | async-start | bytes 4194304 | tf_op jit(solution)/shard_map/all_to_all | solution.py:59
  95.3 0.3 mul.231
  95.7 46.8 %all-to-all-done.1 = f32[2,64,16,256]{3,1,0,2:T(8,128)S(1)} async-done(((f32[2,64,16,256]{3,1,0,2:T(8,128)}), f32[2,64,16,256]{3,1,0,2:T(8,128)S(1)}, u32[]{:S(2)}, u32[]{:S(2)}) %all-to-all-start.1) | async-done | bytes 2097184 | tf_op jit(solution)/shard_map/all_to_all | solution.py:59
  142.7 1.5 %bitcast_multiply_fusion = f32[2,1024,256]{2,1,0:T(8,128)} fusion(f32[2,64,16,256]{3,1,2,0:T(8,128)S(1)} %copy.142, f32[1024,256]{1,0:T(8,128)S(1)} %bitcast.147), kind=kLoop, calls=%fused_computation.1 | loop fusion | flops 524288 | bytes 5242880 | tf_op jit(solution)/shard_map/mul | solution.py:69
  (30 shorter events, 1.3 us)
Async XLA Ops:
  0.0 7.5 %copy-start.4 = (f32[2,1024,256]{2,1,0:T(8,128)S(1)}, f32[2,1024,256]{2,1,0:T(8,128)}, u32[]{:S(2)}) copy-start(f32[2,1024,256]{2,1,0:T(8,128)} %param.4) | copy-start | bytes 6291460
  7.7 1.3 copy-start.3
  9.0 53.9 %all-to-all-start = ((f32[16,2,1,64,256]{4,3,2,1,0:T(8,128)}), f32[16,2,1,64,256]{4,3,2,1,0:T(8,128)S(1)}, u32[]{:S(2)}, u32[]{:S(2)}) async-start(f32[16,2,1,64,256]{4,3,2,1,0:T(8,128)} %bitcast.149), calls=%async_computation | async-start | bytes 4194304 | tf_op jit(solution)/shard_map/all_to_all | solution.py:50
  66.0 3.5 %copy-start.1 = (f32[1,1,64,16,256]{4,2,1,0,3:T(8,128)S(1)}, f32[1,1,64,16,256]{4,2,1,0,3:T(8,128)}, u32[]{:S(2)}) copy-start(f32[1,1,64,16,256]{4,2,1,0,3:T(8,128)} %get-tuple-element.7) | copy-start | bytes 3145732
  74.1 1.3 copy-start
  87.4 1.2 copy-start.2
  90.1 4.9 %copy-start.6 = (s32[8,2]{0,1:T(2,128)S(1)}, s32[8,2]{0,1:T(2,128)}, u32[]{:S(2)}) copy-start(s32[8,2]{0,1:T(2,128)} %param.6) | copy-start | bytes 196
  90.1 4.9 %copy-start.7 = (f32[4]{0:T(128)S(1)}, f32[4]{0:T(128)}, u32[]{:S(2)}) copy-start(f32[4]{0:T(128)} %param.7) | copy-start | bytes 52
  90.1 5.0 %copy-start.5 = (s32[8,2]{0,1:T(2,128)S(1)}, s32[8,2]{0,1:T(2,128)}, u32[]{:S(2)}) copy-start(s32[8,2]{0,1:T(2,128)} %param.5) | copy-start | bytes 196
  90.2 52.3 %all-to-all-start.1 = ((f32[2,64,16,256]{3,1,0,2:T(8,128)}), f32[2,64,16,256]{3,1,0,2:T(8,128)S(1)}, u32[]{:S(2)}, u32[]{:S(2)}) async-start(f32[2,64,16,256]{3,1,0,2:T(8,128)} %pad_maximum_fusion), calls=%async_computation.1 | async-start | bytes 4194304 | tf_op jit(solution)/shard_map/all_to_all | solution.py:59
